TPU v7x, 32 devices: a whole 2x2x4 slice. The times are simulated.
32 devices in a mesh: batch: 8 (over z, x), seq: 4 (over y, core).
Axes of the slice: x: 2, y: 2, z: 4, core: 2. Of those that a mesh axis runs over, the one named last changes fastest.
Arguments:
- tokens: bfloat16 [8, 1024, 1024], P('batch', 'seq'), may hold values from -6 to 6
- cotangent: bfloat16 [8, 1024, 1024], P('batch', 'seq'), may hold values from -6 to 6
- image_tokens: bfloat16 [8, 1025, 768], P('batch'), may hold values from -6 to 6
- image_lengths: int32 [8], P('batch'), may hold values from 512 to 1025, as said below
- key_mask: int32 [8, 1025], P('batch'), may hold values 0 or 1
- camera: bfloat16 [8, 1024], P(None, 'batch'), may hold values from -6 to 6
- modulation: bfloat16 [1024, 6144], P('batch'), may hold values from -0.1875 to 0.1875
- q_cross: bfloat16 [1024, 1024], P('batch'), may hold values from -0.1875 to 0.1875
- kv_image: bfloat16 [768, 2048], P('batch'), may hold values from -0.21875 to 0.21875
- out_cross: bfloat16 [1024, 1024], P('batch'), may hold values from -3.5 to 3.5
- qkv_self: bfloat16 [1024, 3072], P('batch'), may hold values from -0.1875 to 0.1875
- out_self: bfloat16 [1024, 1024], P('batch'), may hold values from -6 to 6
- mlp_in: bfloat16 [1024, 4096], P('batch'), may hold values from -0.1875 to 0.1875
- mlp_out: bfloat16 [4096, 1024], P('batch'), may hold values from -0.09375 to 0.09375
Outputs:
- output: bfloat16 [8, 1024, 1024], P('batch', 'seq')
- grad_tokens: float32 [8, 1024, 1024], P('batch', 'seq')
- grad_modulation: float32 [1024, 6144], P('batch')
- grad_q_cross: float32 [1024, 1024], P('batch')
- grad_kv_image: float32 [768, 2048], P('batch')
- grad_out_cross: float32 [1024, 1024], P('batch')
- grad_qkv_self: float32 [1024, 3072], P('batch')
- grad_out_self: float32 [1024, 1024], P('batch')
- grad_mlp_in: float32 [1024, 4096], P('batch')
- grad_mlp_out: float32 [4096, 1024], P('batch')
Inputs may be any that keep to these rules, and one draw needn't show every extreme that they name: `image_lengths`: some object has 1025 valid image tokens and some has 512.
All inputs are finite; a program needn't handle non-finite values. No bound on the sum of `key_mask` on one device may be relied on, other than what follows from the above.
Results may differ from a plain program's by a relative error of at most 0.025.
The roundings to bfloat16 on the way count: a program that leaves them out, or rounds other values in their place, can miss the bound.
Values may be sent and summed in bfloat16 or wider, within the bound.
A program may use at most 256 MiB of HBM per device.

v0:
```python
import jax
import jax.numpy as jnp
from jax import lax
from jax.sharding import PartitionSpec as P

HEADS = 16
HEAD_DIM = 64
epsilon = 1e-06
group_heads = 4
highest = lax.Precision.HIGHEST


def modulated_norm(values, shift, scale):
    center = values - jnp.mean(values, axis=-1, keepdims=True)
    normed = center * lax.rsqrt(jnp.mean(center * center, axis=-1, keepdims=True) + epsilon)
    return normed * (1.0 + scale) + shift


def product(left, right):
    return jnp.dot(left, right, preferred_element_type=jnp.float32)


def contract_rows(left, right):
    return lax.dot_general(
        left, right, (((0,), (0,)), ((), ())), preferred_element_type=jnp.float32
    )


def times_transposed(left, right):
    return lax.dot_general(
        left, right, (((1,), (1,)), ((), ())), preferred_element_type=jnp.float32
    )


def split_heads(values):
    rows = values.shape[0]
    grouped = values.reshape(rows, HEADS // group_heads, group_heads, HEAD_DIM)
    return grouped.transpose(1, 2, 0, 3)


def join_heads(values):
    groups, inner, rows, depth = values.shape
    return values.transpose(2, 0, 1, 3).reshape(rows, groups * inner * depth)


def scores_of(query_group, key_group, valid):
    scores = jnp.einsum(
        "hqd,hkd->hqk", query_group, key_group, preferred_element_type=jnp.float32
    ) * HEAD_DIM ** (-0.5)
    return jnp.where(valid[None, None, :], scores, -1000000000.0)


def attend_forward(query, key_rows, value_rows, valid):

    def one_group(pieces):
        query_group, key_group, value_group = pieces
        scores = scores_of(query_group, key_group, valid)
        top = jnp.max(scores, axis=-1, keepdims=True)
        expo = jnp.exp(scores - top)
        total = jnp.sum(expo, axis=-1, keepdims=True)
        probs = (expo / total).astype(jnp.bfloat16)
        result = jnp.einsum("hqk,hkd->hqd", probs, value_group, preferred_element_type=jnp.float32)
        return (result, top, total)

    results, tops, totals = lax.map(
        one_group, (split_heads(query), split_heads(key_rows), split_heads(value_rows))
    )
    return (join_heads(results), (tops, totals))


def attend_backward(query, key_rows, value_rows, valid, stats, grad_output):
    tops, totals = stats

    def one_group(pieces):
        query_group, key_group, value_group, top, total, grad_group = pieces
        scores = scores_of(query_group, key_group, valid)
        probs = jnp.exp(scores - top) / total
        grad_probs = jnp.einsum(
            "hqd,hkd->hqk", grad_group, value_group, preferred_element_type=jnp.float32
        )
        inner = jnp.sum(probs * grad_probs, axis=-1, keepdims=True)
        grad_scores = (probs * (grad_probs - inner)).astype(jnp.bfloat16)
        factor = HEAD_DIM ** (-0.5)
        grad_query = (
            jnp.einsum("hqk,hkd->hqd", grad_scores, key_group, preferred_element_type=jnp.float32)
            * factor
        )
        grad_keys = (
            jnp.einsum("hqk,hqd->hkd", grad_scores, query_group, preferred_element_type=jnp.float32)
            * factor
        )
        grad_values = jnp.einsum(
            "hqk,hqd->hkd",
            probs.astype(jnp.bfloat16),
            grad_group,
            preferred_element_type=jnp.float32,
        )
        return (grad_query, inner, grad_keys, grad_values)

    results = lax.map(
        one_group,
        (
            split_heads(query),
            split_heads(key_rows),
            split_heads(value_rows),
            tops,
            totals,
            split_heads(grad_output),
        ),
    )
    return (join_heads(results[0]), results[1], join_heads(results[2]), join_heads(results[3]))


def local(
    tokens,
    cotangent,
    image_tokens,
    image_lengths,
    key_mask,
    camera,
    modulation,
    q_cross,
    kv_image,
    out_cross,
    qkv_self,
    out_self,
    mlp_in,
    mlp_out,
):
    q_full, kv_full, out_cross_full, qkv_full, out_self_full, mlp_in_full, mlp_out_full = (
        lax.all_gather(q_cross, "batch", axis=0, tiled=True),
        lax.all_gather(kv_image, "batch", axis=0, tiled=True),
        lax.all_gather(out_cross, "batch", axis=0, tiled=True),
        lax.all_gather(qkv_self, "batch", axis=0, tiled=True),
        lax.all_gather(out_self, "batch", axis=0, tiled=True),
        lax.all_gather(mlp_in, "batch", axis=0, tiled=True),
        lax.all_gather(mlp_out, "batch", axis=0, tiled=True),
    )
    camera_gate = jax.nn.silu(camera.astype(jnp.float32)).astype(jnp.bfloat16)
    modulation_all = lax.psum(product(camera_gate, modulation), "batch")
    object_index = lax.axis_index("batch")
    width = tokens.shape[2]
    shifts = lax.dynamic_index_in_dim(modulation_all, object_index, 0, keepdims=False).reshape(
        6, width
    )
    stream = tokens[0].astype(jnp.float32)
    image_rows = image_tokens[0]
    positions = jnp.arange(image_rows.shape[0], dtype=jnp.int32)
    valid = (positions < image_lengths[0]) & ((key_mask[0] == 1) | (positions == 0))
    everywhere = jnp.ones((lax.axis_size("seq") * stream.shape[0],), dtype=jnp.bool_)
    normed_cross, cross_pullback = jax.vjp(modulated_norm, stream, shifts[0], shifts[1])
    normed_cross = normed_cross.astype(jnp.bfloat16)
    query_cross = product(normed_cross, q_full).astype(jnp.bfloat16)
    image_kv = product(image_rows, kv_full)
    image_keys = image_kv[:, :width].astype(jnp.bfloat16)
    image_values = image_kv[:, width:].astype(jnp.bfloat16)
    attended_cross, cross_stats = attend_forward(query_cross, image_keys, image_values, valid)
    attended_cross = attended_cross.astype(jnp.bfloat16)
    after_cross = stream + product(attended_cross, out_cross_full)
    normed_self, self_pullback = jax.vjp(modulated_norm, after_cross, shifts[2], shifts[3])
    normed_self = normed_self.astype(jnp.bfloat16)
    packed = product(normed_self, qkv_full).astype(jnp.bfloat16)
    query_self = packed[:, :width]
    key_local = packed[:, width : 2 * width]
    value_local = packed[:, 2 * width :]
    key_whole, value_whole = (
        lax.all_gather(key_local, "seq", axis=0, tiled=True),
        lax.all_gather(value_local, "seq", axis=0, tiled=True),
    )
    attended_self, self_stats = attend_forward(query_self, key_whole, value_whole, everywhere)
    attended_self = attended_self.astype(jnp.bfloat16)
    after_self = after_cross + product(attended_self, out_self_full)
    normed_mlp, mlp_pullback = jax.vjp(modulated_norm, after_self, shifts[4], shifts[5])
    normed_mlp = normed_mlp.astype(jnp.bfloat16)
    up_rows = product(normed_mlp, mlp_in_full)
    hidden, gelu_pullback = jax.vjp(jax.nn.gelu, up_rows)
    hidden = hidden.astype(jnp.bfloat16)
    output = after_self + product(hidden, mlp_out_full)
    grad_stream = cotangent[0].astype(jnp.float32)
    grad_branch = grad_stream.astype(jnp.bfloat16)
    grad_mlp_out = contract_rows(hidden, grad_branch)
    (grad_up,) = gelu_pullback(times_transposed(grad_branch, mlp_out_full))
    grad_up = grad_up.astype(jnp.bfloat16)
    grad_mlp_in = contract_rows(normed_mlp, grad_up)
    grad_from, shift_mlp, scale_mlp = mlp_pullback(times_transposed(grad_up, mlp_in_full))
    grad_stream = grad_stream + grad_from
    grad_branch = grad_stream.astype(jnp.bfloat16)
    grad_out_self = contract_rows(attended_self, grad_branch)
    grad_attended = times_transposed(grad_branch, out_self_full).astype(jnp.bfloat16)
    grad_query, inner_local, key_terms, value_terms = attend_backward(
        query_self, key_whole, value_whole, everywhere, self_stats, grad_attended
    )
    grad_key, grad_value = (
        lax.psum_scatter(key_terms, "seq", scatter_dimension=0, tiled=True),
        lax.psum_scatter(value_terms, "seq", scatter_dimension=0, tiled=True),
    )
    grad_packed = jnp.concatenate([grad_query, grad_key, grad_value], axis=1).astype(jnp.bfloat16)
    grad_qkv_self = contract_rows(normed_self, grad_packed)
    grad_from, shift_self, scale_self = self_pullback(times_transposed(grad_packed, qkv_full))
    grad_stream = grad_stream + grad_from
    grad_branch = grad_stream.astype(jnp.bfloat16)
    grad_out_cross = contract_rows(attended_cross, grad_branch)
    grad_attended = times_transposed(grad_branch, out_cross_full).astype(jnp.bfloat16)
    grad_query, inner_cross, key_terms, value_terms = attend_backward(
        query_cross, image_keys, image_values, valid, cross_stats, grad_attended
    )
    image_float = image_rows.astype(jnp.float32)
    image_key_grad, image_value_grad = (
        lax.psum_scatter(
            key_terms.astype(jnp.bfloat16), "seq", scatter_dimension=1, tiled=True
        ).astype(jnp.float32),
        lax.psum_scatter(
            value_terms.astype(jnp.bfloat16), "seq", scatter_dimension=1, tiled=True
        ).astype(jnp.float32),
    )
    block_width = image_key_grad.shape[1]
    column_start = lax.axis_index("seq") * block_width
    image_grads = jnp.concatenate([image_key_grad, image_value_grad], axis=1)
    kv_block = lax.dot_general(
        image_float,
        image_grads,
        (((0,), (0,)), ((), ())),
        precision=highest,
        preferred_element_type=jnp.float32,
    )
    grad_kv_image = jnp.zeros((image_rows.shape[1], 2 * width), jnp.float32)
    grad_kv_image = lax.dynamic_update_slice(
        grad_kv_image, kv_block[:, :block_width], (jnp.int32(0), column_start)
    )
    grad_kv_image = lax.dynamic_update_slice(
        grad_kv_image, kv_block[:, block_width:], (jnp.int32(0), column_start + width)
    )
    grad_query = grad_query.astype(jnp.bfloat16)
    grad_q_cross = contract_rows(normed_cross, grad_query)
    grad_from, shift_cross, scale_cross = cross_pullback(times_transposed(grad_query, q_full))
    grad_input = grad_stream + grad_from
    grad_row = jnp.concatenate(
        [shift_cross, scale_cross, shift_self, scale_self, shift_mlp, scale_mlp]
    )
    grad_table = lax.dynamic_update_slice(
        jnp.zeros(modulation_all.shape, jnp.float32),
        grad_row[None, :],
        (object_index, jnp.int32(0)),
    )
    grad_table = lax.psum(grad_table, ("batch", "seq"))
    grad_modulation = lax.dot_general(
        camera_gate.astype(jnp.float32),
        grad_table,
        (((0,), (0,)), ((), ())),
        precision=highest,
        preferred_element_type=jnp.float32,
    )
    terms = (
        grad_q_cross,
        grad_kv_image,
        grad_out_cross,
        grad_qkv_self,
        grad_out_self,
        grad_mlp_in,
        grad_mlp_out,
    )
    shares = (
        lax.psum_scatter(
            terms[0].astype(jnp.bfloat16), "batch", scatter_dimension=0, tiled=True
        ).astype(jnp.float32),
        lax.psum_scatter(
            terms[1].astype(jnp.bfloat16), "batch", scatter_dimension=0, tiled=True
        ).astype(jnp.float32),
        lax.psum_scatter(
            terms[2].astype(jnp.bfloat16), "batch", scatter_dimension=0, tiled=True
        ).astype(jnp.float32),
        lax.psum_scatter(
            terms[3].astype(jnp.bfloat16), "batch", scatter_dimension=0, tiled=True
        ).astype(jnp.float32),
        lax.psum_scatter(
            terms[4].astype(jnp.bfloat16), "batch", scatter_dimension=0, tiled=True
        ).astype(jnp.float32),
        lax.psum_scatter(
            terms[5].astype(jnp.bfloat16), "batch", scatter_dimension=0, tiled=True
        ).astype(jnp.float32),
        lax.psum_scatter(
            terms[6].astype(jnp.bfloat16), "batch", scatter_dimension=0, tiled=True
        ).astype(jnp.float32),
    )
    totals = (
        lax.psum(shares[0].astype(jnp.bfloat16), "seq").astype(jnp.float32),
        lax.psum(shares[1].astype(jnp.bfloat16), "seq").astype(jnp.float32),
        lax.psum(shares[2].astype(jnp.bfloat16), "seq").astype(jnp.float32),
        lax.psum(shares[3].astype(jnp.bfloat16), "seq").astype(jnp.float32),
        lax.psum(shares[4].astype(jnp.bfloat16), "seq").astype(jnp.float32),
        lax.psum(shares[5].astype(jnp.bfloat16), "seq").astype(jnp.float32),
        lax.psum(shares[6].astype(jnp.bfloat16), "seq").astype(jnp.float32),
    )
    return (
        output.astype(jnp.bfloat16)[None],
        grad_input[None],
        grad_modulation,
        totals[0],
        totals[1],
        totals[2],
        totals[3],
        totals[4],
        totals[5],
        totals[6],
    )


def solution(mesh):
    return jax.shard_map(
        local,
        mesh=mesh,
        in_specs=(
            P("batch", "seq", None),
            P("batch", "seq", None),
            P("batch", None, None),
            P("batch"),
            P("batch", None),
            P(None, "batch"),
            P("batch", None),
            P("batch", None),
            P("batch", None),
            P("batch", None),
            P("batch", None),
            P("batch", None),
            P("batch", None),
            P("batch", None),
        ),
        out_specs=(
            P("batch", "seq", None),
            P("batch", "seq", None),
            P("batch", None),
            P("batch", None),
            P("batch", None),
            P("batch", None),
            P("batch", None),
            P("batch", None),
            P("batch", None),
            P("batch", None),
        ),
        check_vma=False,
    )
```

profile of v0, /device:TPU:0, one launch (start us, length us, event | category | flops | bytes accessed | tf_op | source)
XLA Modules:
  0.0 1926.2 jit_solution(18248695921334428257)
XLA Ops:
  15.5 69.2 %all-reduce.5.cloned.1.call-done = f32[8,6144]{1,0:T(8,128)} async-done(((f32[8,6144]{1,0:T(8,128)}), f32[8,6144]{1,0:T(8,128)}) %all-reduce.5.cloned.1.call-update) | async-done | bytes 196624 | tf_op jit(solution)/shard_map/psum | solution.py:140
  85.7 49.7 %all-gather.10.cloned.1.call-done = bf16[1024,1024]{1,0:T(8,128)(2,1)} async-done(((bf16[128,1024]{1,0:T(8,128)(2,1)}), bf16[1024,1024]{1,0:T(8,128)(2,1)}) %all-gather.10.cloned.1.call-update) | async-done | bytes 2097168 | tf_op jit(solution)/shard_map/all_gather | solution.py:131
  138.0 58.8 %all-gather.12.cloned.1.call-done = bf16[768,2048]{1,0:T(8,128)(2,1)} async-done(((bf16[96,2048]{1,0:T(8,128)(2,1)}), bf16[768,2048]{1,0:T(8,128)(2,1)}) %all-gather.12.cloned.1.call-update) | async-done | bytes 3145744 | tf_op jit(solution)/shard_map/all_gather | solution.py:132
  213.2 18.4 while.56
  231.7 15.3 all-gather.14.cloned.1.call-done
  249.9 96.9 %all-gather.16.cloned.1.call-done = bf16[1024,3072]{1,0:T(8,128)(2,1)} async-done(((bf16[128,3072]{1,0:T(8,128)(2,1)}), bf16[1024,3072]{1,0:T(8,128)(2,1)}) %all-gather.16.cloned.1.call-update) | async-done | bytes 6291472 | tf_op jit(solution)/shard_map/all_gather | solution.py:134
  357.0 16.6 all-gather.18.cloned.1.call-done
  377.6 20.9 %all-gather.20.cloned.1.call-done = bf16[1024,1024]{1,0:T(8,128)(2,1)} async-done(((bf16[256,1024]{1,0:T(8,128)(2,1)}), bf16[1024,1024]{1,0:T(8,128)(2,1)}) %all-gather.20.cloned.1.call-update) | async-done | bytes 2097168 | tf_op jit(solution)/shard_map/all_gather | solution.py:168
  403.3 23.0 %while.57 = (s32[]{:T(128)}, bf16[4,4,256,64]{2,3,1,0:T(8,128)(2,1)}, f32[4,4,256,1]{2,1,3,0:T(4,128)S(1)}, f32[4,4,256,1]{2,1,3,0:T(4,128)S(1)}, bf16[4,4,256,6...) while((s32[]{:T(128)}, ...), condition=%wide.region_12.13_spmd, body=%wide.region_9.12_spmd.sunk | while | flops 277870592 | bytes 18258072 | solution.py:65
  426.2 24.1 %all-gather.22.cloned.1.call-done = bf16[1024,1024]{1,0:T(8,128)(2,1)} async-done(((bf16[128,1024]{1,0:T(8,128)(2,1)}), bf16[1024,1024]{1,0:T(8,128)(2,1)}) %all-gather.22.cloned.1.call-update) | async-done | bytes 2097168 | tf_op jit(solution)/shard_map/all_gather | solution.py:135
  454.2 122.0 %all-gather.24.cloned.1.call-done = bf16[1024,4096]{1,0:T(8,128)(2,1)} async-done(((bf16[128,4096]{1,0:T(8,128)(2,1)}), bf16[1024,4096]{1,0:T(8,128)(2,1)}) %all-gather.24.cloned.1.call-update) | async-done | bytes 8388624 | tf_op jit(solution)/shard_map/all_gather | solution.py:136
  576.2 8.1 fusion.160
  584.3 117.2 %all-gather.26.cloned.1.call-done = bf16[4096,1024]{1,0:T(8,128)(2,1)} async-done(((bf16[512,1024]{1,0:T(8,128)(2,1)}), bf16[4096,1024]{1,0:T(8,128)(2,1)}) %all-gather.26.cloned.1.call-update) | async-done | bytes 8388624 | tf_op jit(solution)/shard_map/all_gather | solution.py:137
  701.5 9.3 fusion.95
  720.9 39.8 %while.58 = (s32[]{:T(128)}, bf16[4,4,256,64]{2,3,1,0:T(8,128)(2,1)}, f32[4,4,1024,64]{2,3,1,0:T(8,128)}, f32[4,4,1024,64]{2,3,1,0:T(8,128)}, bf16[4,4,256,64]{2...) while((s32[]{:T(128)}, ...), condition=%wide.region_19.20_spmd, body=%wide.region_17.19_spmd.sunk | while | flops 680852480 | bytes 48534732 | solution.py:100
  761.4 42.2 %reduce-scatter.14.cloned.1.call-done = f32[256,1024]{0,1:T(8,128)} async-done(((f32[1024,1024]{0,1:T(8,128)}), f32[256,1024]{0,1:T(8,128)}) %reduce-scatter.14.cloned.1.call-update) | async-done | bytes 1048592 | tf_op jit(solution)/shard_map/reduce_scatter | solution.py:195
  804.9 45.6 %reduce-scatter.12.cloned.1.call-done = f32[256,1024]{0,1:T(8,128)} async-done(((f32[1024,1024]{0,1:T(8,128)}), f32[256,1024]{0,1:T(8,128)}) %reduce-scatter.12.cloned.1.call-update) | async-done | bytes 1048592 | tf_op jit(solution)/shard_map/reduce_scatter | solution.py:194
  863.9 40.3 %while.59 = (s32[]{:T(128)}, bf16[4,4,256,64]{2,3,1,0:T(8,128)(2,1)}, bf16[4,4,1025,64]{2,3,1,0:T(8,128)(2,1)}, bf16[4,4,1025,64]{2,3,1,0:T(8,128)(2,1)}, pred[1...) while((s32[]{:T(128)}, ...), condition=%wide.region_26.27_spmd, body=%wide.region_24.26_spmd.sunk | while | flops 682566912 | bytes 82707776 | solution.py:100
  915.6 7.7 convolution_convert_fusion.1
  923.4 8.6 convolution_convert_fusion
  937.4 35.5 %reduce-scatter.18.cloned.1.call-done = bf16[1025,256]{0,1:T(8,128)(2,1)} async-done(((bf16[1025,1024]{0,1:T(8,128)(2,1)}), bf16[1025,256]{0,1:T(8,128)(2,1)}) %reduce-scatter.18.cloned.1.call-update) | async-done | bytes 524816 | tf_op jit(solution)/shard_map/reduce_scatter | solution.py:209
  982.9 6.3 convolution_convert_fusion.3
  995.6 48.8 %reduce-scatter.28.cloned.1.call-done = bf16[128,1024]{1,0:T(8,128)(2,1)} async-done(((bf16[1024,1024]{1,0:T(8,128)(2,1)}), bf16[128,1024]{1,0:T(8,128)(2,1)}) %reduce-scatter.28.cloned.1.call-update) | async-done | bytes 262160 | tf_op jit(solution)/shard_map/reduce_scatter | solution.py:275
  1044.4 71.2 %reduce-scatter.16.cloned.1.call-done = bf16[128,1024]{1,0:T(8,128)(2,1)} async-done(((bf16[1024,1024]{1,0:T(8,128)(2,1)}), bf16[128,1024]{1,0:T(8,128)(2,1)}) %reduce-scatter.16.cloned.1.call-update) | async-done | bytes 262160 | tf_op jit(solution)/shard_map/reduce_scatter | solution.py:263
  1115.6 71.3 %reduce-scatter.24.cloned.1.call-done = bf16[128,1024]{1,0:T(8,128)(2,1)} async-done(((bf16[1024,1024]{1,0:T(8,128)(2,1)}), bf16[128,1024]{1,0:T(8,128)(2,1)}) %reduce-scatter.24.cloned.1.call-update) | async-done | bytes 262160 | tf_op jit(solution)/shard_map/reduce_scatter | solution.py:269
  1186.9 152.0 %reduce-scatter.30.cloned.1.call-done = bf16[128,4096]{1,0:T(8,128)(2,1)} async-done(((bf16[1024,4096]{1,0:T(8,128)(2,1)}), bf16[128,4096]{1,0:T(8,128)(2,1)}) %reduce-scatter.30.cloned.1.call-update) | async-done | bytes 1048592 | tf_op jit(solution)/shard_map/reduce_scatter | solution.py:278
  1338.9 151.7 %reduce-scatter.32.cloned.1.call-done = bf16[512,1024]{1,0:T(8,128)(2,1)} async-done(((bf16[4096,1024]{1,0:T(8,128)(2,1)}), bf16[512,1024]{1,0:T(8,128)(2,1)}) %reduce-scatter.32.cloned.1.call-update) | async-done | bytes 1048592 | tf_op jit(solution)/shard_map/reduce_scatter | solution.py:281
  1490.6 77.8 %reduce-scatter.22.cloned.1.call-done = bf16[96,2048]{1,0:T(8,128)(2,1)} async-done(((bf16[768,2048]{1,0:T(8,128)(2,1)}), bf16[96,2048]{1,0:T(8,128)(2,1)}) %reduce-scatter.22.cloned.1.call-update) | async-done | bytes 393232 | tf_op jit(solution)/shard_map/reduce_scatter | solution.py:266
  1568.4 121.2 %reduce-scatter.26.cloned.1.call-done = bf16[128,3072]{1,0:T(8,128)(2,1)} async-done(((bf16[1024,3072]{1,0:T(8,128)(2,1)}), bf16[128,3072]{1,0:T(8,128)(2,1)}) %reduce-scatter.26.cloned.1.call-update) | async-done | bytes 786448 | tf_op jit(solution)/shard_map/reduce_scatter | solution.py:272
  1689.7 8.3 fusion.108
  1699.4 119.4 %all-reduce.7.cloned.1.call-done = f32[8,6144]{1,0:T(8,128)} async-done(((f32[8,6144]{1,0:T(8,128)}), f32[8,6144]{1,0:T(8,128)}) %all-reduce.7.cloned.1.call-update) | async-done | bytes 196624 | tf_op jit(solution)/shard_map/psum | solution.py:245
  1822.9 84.5 %all-reduce.9.cloned.1.call-done = (bf16[128,1024]{1,0:T(8,128)(2,1)}, bf16[96,2048]{1,0:T(8,128)(2,1)}, bf16[128,1024]{1,0:T(8,128)(2,1)}, bf16[128,3072]{1,0:T...) async-done(((bf16[128,1024]{1,0:T(8,128)(2,1)}, bf16[96,2048]{1,0:T(8,128)(2,1)}, bf16[128,1024]{1,0:T(8,128)(2,1)}, ...) | async-done | bytes 4063248 | tf_op jit(solution)/shard_map/psum | solution.py:286
  (435 shorter events, 248.7 us)
Async XLA Ops:
  7.2 189.7 %copy-start = (bf16[1,1025,768]{2,1,0:T(8,128)(2,1)S(1)}, bf16[1,1025,768]{2,1,0:T(8,128)(2,1)}, u32[]{:S(2)}) copy-start(bf16[1,1025,768]{2,1,0:T(8,128)(2,1)} %param.24) | copy-start | bytes 4723204
  7.2 77.5 %all-reduce.5.cloned.1.call-start = ((), (), s32[]{:S(2)}) async-start(), calls=%async_computation.11 | async-start | bytes 393216 | tf_op jit(solution)/shard_map/psum | solution.py:140
  9.8 125.6 %all-gather.10.cloned.1.call-start = ((), (), s32[]{:S(2)}) async-start(), calls=%async_computation.12 | async-start | bytes 2359296 | tf_op jit(solution)/shard_map/all_gather | solution.py:131
  10.6 186.2 %all-gather.12.cloned.1.call-start = ((), (), s32[]{:S(2)}) async-start(), calls=%async_computation.13 | async-start | bytes 3538944 | tf_op jit(solution)/shard_map/all_gather | solution.py:132
  11.3 235.6 %all-gather.14.cloned.1.call-start = ((), (), s32[]{:S(2)}) async-start(), calls=%async_computation.14 | async-start | bytes 2359296 | tf_op jit(solution)/shard_map/all_gather | solution.py:133
  11.9 334.9 %all-gather.16.cloned.1.call-start = ((), (), s32[]{:S(2)}) async-start(), calls=%async_computation.15 | async-start | bytes 7077888 | tf_op jit(solution)/shard_map/all_gather | solution.py:134
  12.5 361.1 %all-gather.18.cloned.1.call-start = ((), (), s32[]{:S(2)}) async-start(), calls=%async_computation.16 | async-start | bytes 2621440 | tf_op jit(solution)/shard_map/all_gather | solution.py:167
  85.7 261.1 %copy-start.41 = (f32[1,1024]{1,0:T(1,128)}, f32[1,1024]{1,0:T(1,128)S(1)}, u32[]{:S(2)}) copy-start(f32[1,1024]{1,0:T(1,128)S(1)} %get-tuple-element.334) | copy-start | bytes 12292
  85.7 490.5 %copy-start.42 = (f32[1,1024]{1,0:T(1,128)}, f32[1,1024]{1,0:T(1,128)S(1)}, u32[]{:S(2)}) copy-start(f32[1,1024]{1,0:T(1,128)S(1)} %get-tuple-element.338) | copy-start | bytes 12292
  85.7 628.4 %copy-start.39 = (f32[1,1024]{1,0:T(1,128)}, f32[1,1024]{1,0:T(1,128)S(1)}, u32[]{:S(2)}) copy-start(f32[1,1024]{1,0:T(1,128)S(1)} %get-tuple-element.333) | copy-start | bytes 12292
  249.6 608.1 %copy-start.52 = (f32[256]{0:T(256)}, f32[256]{0:T(256)S(1)}, u32[]{:S(2)}) copy-start(f32[256]{0:T(256)S(1)} %broadcast_multiply_fusion.1) | copy-start | bytes 3076
  249.9 607.8 %copy-start.58 = (f32[256]{0:T(256)}, f32[256]{0:T(256)S(1)}, u32[]{:S(2)}) copy-start(f32[256]{0:T(256)S(1)} %fusion.150) | copy-start | bytes 3076
  352.7 45.8 %all-gather.20.cloned.1.call-start = ((), (), s32[]{:S(2)}) async-start(), calls=%async_computation.17 | async-start | bytes 2621440 | tf_op jit(solution)/shard_map/all_gather | solution.py:168
  353.4 96.9 %all-gather.22.cloned.1.call-start = ((), (), s32[]{:S(2)}) async-start(), calls=%async_computation.18 | async-start | bytes 2359296 | tf_op jit(solution)/shard_map/all_gather | solution.py:135
  354.2 222.0 %all-gather.24.cloned.1.call-start = ((), (), s32[]{:S(2)}) async-start(), calls=%async_computation.19 | async-start | bytes 9437184 | tf_op jit(solution)/shard_map/all_gather | solution.py:136
  354.9 346.6 %all-gather.26.cloned.1.call-start = ((), (), s32[]{:S(2)}) async-start(), calls=%async_computation.20 | async-start | bytes 9437184 | tf_op jit(solution)/shard_map/all_gather | solution.py:137
  355.5 448.1 %reduce-scatter.14.cloned.1.call-start = ((), (), s32[]{:S(2)}) async-start(), calls=%async_computation.22 | async-start | bytes 5242880 | tf_op jit(solution)/shard_map/reduce_scatter | solution.py:195
  453.0 261.1 %copy-start.53 = (f32[256]{0:T(256)}, f32[256]{0:T(256)S(1)}, u32[]{:S(2)}) copy-start(f32[256]{0:T(256)S(1)} %broadcast_multiply_fusion) | copy-start | bytes 3076
  454.2 259.9 %copy-start.59 = (f32[256]{0:T(256)}, f32[256]{0:T(256)S(1)}, u32[]{:S(2)}) copy-start(f32[256]{0:T(256)S(1)} %fusion.151) | copy-start | bytes 3076
  760.8 89.7 %reduce-scatter.12.cloned.1.call-start = ((), (), s32[]{:S(2)}) async-start(), calls=%async_computation.21 | async-start | bytes 5242880 | tf_op jit(solution)/shard_map/reduce_scatter | solution.py:194
  761.3 176.1 %reduce-scatter.20.cloned.1.call-start = ((), (), s32[]{:S(2)}) async-start(), calls=%async_computation.26 | async-start | bytes 2949120 | tf_op jit(solution)/shard_map/reduce_scatter | solution.py:212
  904.3 68.7 %reduce-scatter.18.cloned.1.call-start = ((), (), s32[]{:S(2)}) async-start(), calls=%async_computation.25 | async-start | bytes 2949120 | tf_op jit(solution)/shard_map/reduce_scatter | solution.py:209
  904.9 139.5 %reduce-scatter.28.cloned.1.call-start = ((), (), s32[]{:S(2)}) async-start(), calls=%async_computation.30 | async-start | bytes 2359296 | tf_op jit(solution)/shard_map/reduce_scatter | solution.py:275
  908.2 207.4 %reduce-scatter.16.cloned.1.call-start = ((), (), s32[]{:S(2)}) async-start(), calls=%async_computation.24 | async-start | bytes 2359296 | tf_op jit(solution)/shard_map/reduce_scatter | solution.py:263
  911.8 275.1 %reduce-scatter.24.cloned.1.call-start = ((), (), s32[]{:S(2)}) async-start(), calls=%async_computation.28 | async-start | bytes 2359296 | tf_op jit(solution)/shard_map/reduce_scatter | solution.py:269
  915.5 423.4 %reduce-scatter.30.cloned.1.call-start = ((), (), s32[]{:S(2)}) async-start(), calls=%async_computation.31 | async-start | bytes 9437184 | tf_op jit(solution)/shard_map/reduce_scatter | solution.py:278
  923.3 567.3 %reduce-scatter.32.cloned.1.call-start = ((), (), s32[]{:S(2)}) async-start(), calls=%async_computation.32 | async-start | bytes 9437184 | tf_op jit(solution)/shard_map/reduce_scatter | solution.py:281
  932.0 636.4 %reduce-scatter.22.cloned.1.call-start = ((), (), s32[]{:S(2)}) async-start(), calls=%async_computation.27 | async-start | bytes 3538944 | tf_op jit(solution)/shard_map/reduce_scatter | solution.py:266
  982.9 706.8 %reduce-scatter.26.cloned.1.call-start = ((), (), s32[]{:S(2)}) async-start(), calls=%async_computation.29 | async-start | bytes 7077888 | tf_op jit(solution)/shard_map/reduce_scatter | solution.py:272
  989.3 700.4 %copy-start.5 = (f32[256,1024]{1,0:T(8,128)S(1)}, f32[256,1024]{1,0:T(8,128)}, u32[]{:S(2)}) copy-start(f32[256,1024]{1,0:T(8,128)} %copy-done.3) | copy-start | bytes 3145732
  989.3 829.5 %all-reduce.7.cloned.1.call-start = ((), (), s32[]{:S(2)}) async-start(), calls=%async_computation.23 | async-start | bytes 393216 | tf_op jit(solution)/shard_map/psum | solution.py:245
  995.5 911.8 %all-reduce.9.cloned.1.call-start = ((), (), s32[]{:S(2)}) async-start(), calls=%async_computation.33 | async-start | bytes 8126464 | tf_op jit(solution)/shard_map/psum | solution.py:286
  (98 other events, 1340.5 us)
Sparse Core Ops, SparseCore 0:
  11.9 72.7 all-reduce.4
  87.1 48.3 all-gather.9
  137.9 58.9 all-gather.11
  199.0 47.9 all-gather.13
  249.2 97.5 all-gather.15
  352.8 20.7 all-gather.17
  375.8 22.5 all-gather.19
  400.8 49.5 all-gather.21
  452.7 123.4 all-gather.23
  578.4 123.1 all-gather.25
  760.9 42.6 reduce-scatter.13
  806.0 44.4 reduce-scatter.11
  904.3 33.0 reduce-scatter.19
  939.8 33.0 reduce-scatter.17
  976.7 67.6 reduce-scatter.27
  1048.8 66.7 reduce-scatter.15
  1120.0 66.8 reduce-scatter.23
  1190.8 148.0 reduce-scatter.29
  1342.5 147.9 reduce-scatter.31
  1495.0 73.3 reduce-scatter.21
  1572.4 117.1 reduce-scatter.25
  1696.7 122.1 all-reduce.6
  1822.0 85.3 all-reduce.8
where the time goes:
time: 1940 us; the launch traced here: 1930 us
  waiting for transfers between devices  1620 us (84%)
  matrix products  195 us (10%)
  local copies, waits for them, and re-layouts  57.6 us (3%)
  other arithmetic  31.7 us (2%)
    reduce_scatter x1, waiting for transfers between devices, local(): lax.psum_scatter(terms[5].astype(jnp.bfloat16), 'batch', scatter_dimensio...  152 us
    reduce_scatter x1, waiting for transfers between devices, local(): lax.psum_scatter(terms[6].astype(jnp.bfloat16), 'batch', scatter_dimensio...  152 us
    all_gather x1, waiting for transfers between devices, local(): lax.all_gather(mlp_in, 'batch', axis=0, tiled=True)  122 us
    reduce_scatter x1, waiting for transfers between devices, local(): lax.psum_scatter(terms[3].astype(jnp.bfloat16), 'batch', scatter_dimensio...  121 us
    psum x1, waiting for transfers between devices, local(): grad_table = lax.psum(grad_table, ('batch', 'seq'))  119 us
    all_gather x1, waiting for transfers between devices, local(): lax.all_gather(mlp_out, 'batch', axis=0, tiled=True)  117 us
    all_gather x1, waiting for transfers between devices, local(): lax.all_gather(qkv_self, 'batch', axis=0, tiled=True)  96.9 us
    psum x1, waiting for transfers between devices, local(): lax.psum(shares[0].astype(jnp.bfloat16), 'seq').astype(jnp.float32)  84.5 us
  transfers between devices with their start and end apart: 23, of which 23 were waited for; matrix products, arithmetic and copies ran while one was open for 8% of the time, Pallas kernels for 0%

commit v1 on v0

--- a/solution.py
+++ b/solution.py
@@ -1,3 +1,4 @@
+import functools
 import jax
 import jax.numpy as jnp
 from jax import lax
@@ -8,6 +9,13 @@
 epsilon = 1e-06
 group_heads = 4
 highest = lax.Precision.HIGHEST
+
+
+def review_the_copies(x_in, dev_axis):
+    return jnp.sum(lax.all_gather(x_in, dev_axis), axis=0)
+
+
+part_thing_here = functools.partial(review_the_copies, dev_axis="seq")
 
 
 def modulated_norm(values, shift, scale):
@@ -283,7 +291,7 @@
         ).astype(jnp.float32),
     )
     totals = (
-        lax.psum(shares[0].astype(jnp.bfloat16), "seq").astype(jnp.float32),
+        part_thing_here(shares[0].astype(jnp.bfloat16)).astype(jnp.float32),
         lax.psum(shares[1].astype(jnp.bfloat16), "seq").astype(jnp.float32),
         lax.psum(shares[2].astype(jnp.bfloat16), "seq").astype(jnp.float32),
         lax.psum(shares[3].astype(jnp.bfloat16), "seq").astype(jnp.float32),

time: 1940 us -> 1950 us (level)
    reduce_scatter x1, waiting for transfers between devices: 48.8 us -> 70.6 us  [local(): lax.psum_scatter(terms[4].astype(jnp.bfloat16), 'batch', scatter_dimensio...]
    reduce_scatter x1, waiting for transfers between devices: 71.2 us -> 49.5 us  [local(): lax.psum_scatter(terms[0].astype(jnp.bfloat16), 'batch', scatter_dimensio...]
  transfers between devices with their start and end apart: 23 -> 24, of which waited for: 23 -> 24; matrix products, arithmetic and copies ran while one was open for 8% -> 8% of each run, Pallas kernels for 0% -> 0%
where the time goes in v1:
time: 1950 us; the launch traced here: 1940 us
  waiting for transfers between devices  1630 us (84%)
  matrix products  195 us (10%)
  local copies, waits for them, and re-layouts  57.9 us (3%)
  other arithmetic  32.1 us (2%)
    reduce_scatter x1, waiting for transfers between devices, local(): lax.psum_scatter(terms[5].astype(jnp.bfloat16), 'batch', scatter_dimensio...  152 us
    reduce_scatter x1, waiting for transfers between devices, local(): lax.psum_scatter(terms[6].astype(jnp.bfloat16), 'batch', scatter_dimensio...  152 us
    all_gather x1, waiting for transfers between devices, local(): lax.all_gather(mlp_in, 'batch', axis=0, tiled=True)  122 us
    reduce_scatter x1, waiting for transfers between devices, local(): lax.psum_scatter(terms[3].astype(jnp.bfloat16), 'batch', scatter_dimensio...  121 us
    psum x1, waiting for transfers between devices, local(): grad_table = lax.psum(grad_table, ('batch', 'seq'))  119 us
    all_gather x1, waiting for transfers between devices, local(): lax.all_gather(mlp_out, 'batch', axis=0, tiled=True)  117 us
    all_gather x1, waiting for transfers between devices, local(): lax.all_gather(qkv_self, 'batch', axis=0, tiled=True)  96.9 us
    psum x1, waiting for transfers between devices, local(): lax.psum(shares[1].astype(jnp.bfloat16), 'seq').astype(jnp.float32)  80.6 us
  transfers between devices with their start and end apart: 24, of which 24 were waited for; matrix products, arithmetic and copies ran while one was open for 8% of the time, Pallas kernels for 0%

profile of v1, /device:TPU:0, one launch (start us, length us, event | category | flops | bytes accessed | tf_op | source)
XLA Modules:
  0.0 1938.4 jit_solution(13779485756038650673)
XLA Ops:
  15.5 69.2 %all-reduce.5.cloned.1.call-done = f32[8,6144]{1,0:T(8,128)} async-done(((f32[8,6144]{1,0:T(8,128)}), f32[8,6144]{1,0:T(8,128)}) %all-reduce.5.cloned.1.call-update) | async-done | bytes 196624 | tf_op jit(solution)/shard_map/psum | solution.py:148
  85.7 49.7 %all-gather.12.cloned.1.call-done = bf16[1024,1024]{1,0:T(8,128)(2,1)} async-done(((bf16[128,1024]{1,0:T(8,128)(2,1)}), bf16[1024,1024]{1,0:T(8,128)(2,1)}) %all-gather.12.cloned.1.call-update) | async-done | bytes 2097168 | tf_op jit(solution)/shard_map/all_gather | solution.py:139
  138.0 58.8 %all-gather.14.cloned.1.call-done = bf16[768,2048]{1,0:T(8,128)(2,1)} async-done(((bf16[96,2048]{1,0:T(8,128)(2,1)}), bf16[768,2048]{1,0:T(8,128)(2,1)}) %all-gather.14.cloned.1.call-update) | async-done | bytes 3145744 | tf_op jit(solution)/shard_map/all_gather | solution.py:140
  213.2 18.4 while.56
  231.7 15.3 all-gather.16.cloned.1.call-done
  249.9 96.9 %all-gather.18.cloned.1.call-done = bf16[1024,3072]{1,0:T(8,128)(2,1)} async-done(((bf16[128,3072]{1,0:T(8,128)(2,1)}), bf16[1024,3072]{1,0:T(8,128)(2,1)}) %all-gather.18.cloned.1.call-update) | async-done | bytes 6291472 | tf_op jit(solution)/shard_map/all_gather | solution.py:142
  357.0 16.6 all-gather.20.cloned.1.call-done
  377.6 20.9 %all-gather.22.cloned.1.call-done = bf16[1024,1024]{1,0:T(8,128)(2,1)} async-done(((bf16[256,1024]{1,0:T(8,128)(2,1)}), bf16[1024,1024]{1,0:T(8,128)(2,1)}) %all-gather.22.cloned.1.call-update) | async-done | bytes 2097168 | tf_op jit(solution)/shard_map/all_gather | solution.py:176
  403.3 23.0 %while.57 = (s32[]{:T(128)}, bf16[4,4,256,64]{2,3,1,0:T(8,128)(2,1)}, f32[4,4,256,1]{2,1,3,0:T(4,128)S(1)}, f32[4,4,256,1]{2,1,3,0:T(4,128)S(1)}, bf16[4,4,256,6...) while((s32[]{:T(128)}, ...), condition=%wide.region_12.13_spmd, body=%wide.region_9.12_spmd.sunk | while | flops 277870592 | bytes 18258072 | solution.py:73
  426.2 24.1 %all-gather.24.cloned.1.call-done = bf16[1024,1024]{1,0:T(8,128)(2,1)} async-done(((bf16[128,1024]{1,0:T(8,128)(2,1)}), bf16[1024,1024]{1,0:T(8,128)(2,1)}) %all-gather.24.cloned.1.call-update) | async-done | bytes 2097168 | tf_op jit(solution)/shard_map/all_gather | solution.py:143
  454.2 122.0 %all-gather.26.cloned.1.call-done = bf16[1024,4096]{1,0:T(8,128)(2,1)} async-done(((bf16[128,4096]{1,0:T(8,128)(2,1)}), bf16[1024,4096]{1,0:T(8,128)(2,1)}) %all-gather.26.cloned.1.call-update) | async-done | bytes 8388624 | tf_op jit(solution)/shard_map/all_gather | solution.py:144
  576.2 8.1 fusion.160
  584.3 117.2 %all-gather.28.cloned.1.call-done = bf16[4096,1024]{1,0:T(8,128)(2,1)} async-done(((bf16[512,1024]{1,0:T(8,128)(2,1)}), bf16[4096,1024]{1,0:T(8,128)(2,1)}) %all-gather.28.cloned.1.call-update) | async-done | bytes 8388624 | tf_op jit(solution)/shard_map/all_gather | solution.py:145
  701.5 9.3 fusion.95
  720.9 39.8 %while.58 = (s32[]{:T(128)}, bf16[4,4,256,64]{2,3,1,0:T(8,128)(2,1)}, f32[4,4,1024,64]{2,3,1,0:T(8,128)}, f32[4,4,1024,64]{2,3,1,0:T(8,128)}, bf16[4,4,256,64]{2...) while((s32[]{:T(128)}, ...), condition=%wide.region_19.20_spmd, body=%wide.region_17.19_spmd.sunk | while | flops 680852480 | bytes 48534732 | solution.py:108
  761.4 42.2 %reduce-scatter.14.cloned.1.call-done = f32[256,1024]{0,1:T(8,128)} async-done(((f32[1024,1024]{0,1:T(8,128)}), f32[256,1024]{0,1:T(8,128)}) %reduce-scatter.14.cloned.1.call-update) | async-done | bytes 1048592 | tf_op jit(solution)/shard_map/reduce_scatter | solution.py:203
  804.9 45.6 %reduce-scatter.12.cloned.1.call-done = f32[256,1024]{0,1:T(8,128)} async-done(((f32[1024,1024]{0,1:T(8,128)}), f32[256,1024]{0,1:T(8,128)}) %reduce-scatter.12.cloned.1.call-update) | async-done | bytes 1048592 | tf_op jit(solution)/shard_map/reduce_scatter | solution.py:202
  863.9 40.3 %while.59 = (s32[]{:T(128)}, bf16[4,4,256,64]{2,3,1,0:T(8,128)(2,1)}, bf16[4,4,1025,64]{2,3,1,0:T(8,128)(2,1)}, bf16[4,4,1025,64]{2,3,1,0:T(8,128)(2,1)}, pred[1...) while((s32[]{:T(128)}, ...), condition=%wide.region_26.27_spmd, body=%wide.region_24.26_spmd.sunk | while | flops 682566912 | bytes 82707776 | solution.py:108
  916.0 7.7 convolution_convert_fusion.1
  923.7 8.6 convolution_convert_fusion
  937.4 35.5 %reduce-scatter.18.cloned.1.call-done = bf16[1025,256]{0,1:T(8,128)(2,1)} async-done(((bf16[1025,1024]{0,1:T(8,128)(2,1)}), bf16[1025,256]{0,1:T(8,128)(2,1)}) %reduce-scatter.18.cloned.1.call-update) | async-done | bytes 524816 | tf_op jit(solution)/shard_map/reduce_scatter | solution.py:217
  995.5 49.5 %reduce-scatter.16.cloned.1.call-done = bf16[128,1024]{1,0:T(8,128)(2,1)} async-done(((bf16[1024,1024]{1,0:T(8,128)(2,1)}), bf16[128,1024]{1,0:T(8,128)(2,1)}) %reduce-scatter.16.cloned.1.call-update) | async-done | bytes 262160 | tf_op jit(solution)/shard_map/reduce_scatter | solution.py:271
  1045.0 70.6 %reduce-scatter.28.cloned.1.call-done = bf16[128,1024]{1,0:T(8,128)(2,1)} async-done(((bf16[1024,1024]{1,0:T(8,128)(2,1)}), bf16[128,1024]{1,0:T(8,128)(2,1)}) %reduce-scatter.28.cloned.1.call-update) | async-done | bytes 262160 | tf_op jit(solution)/shard_map/reduce_scatter | solution.py:283
  1115.6 71.3 %reduce-scatter.24.cloned.1.call-done = bf16[128,1024]{1,0:T(8,128)(2,1)} async-done(((bf16[1024,1024]{1,0:T(8,128)(2,1)}), bf16[128,1024]{1,0:T(8,128)(2,1)}) %reduce-scatter.24.cloned.1.call-update) | async-done | bytes 262160 | tf_op jit(solution)/shard_map/reduce_scatter | solution.py:277
  1186.8 152.0 %reduce-scatter.30.cloned.1.call-done = bf16[128,4096]{1,0:T(8,128)(2,1)} async-done(((bf16[1024,4096]{1,0:T(8,128)(2,1)}), bf16[128,4096]{1,0:T(8,128)(2,1)}) %reduce-scatter.30.cloned.1.call-update) | async-done | bytes 1048592 | tf_op jit(solution)/shard_map/reduce_scatter | solution.py:286
  1338.9 151.7 %reduce-scatter.32.cloned.1.call-done = bf16[512,1024]{1,0:T(8,128)(2,1)} async-done(((bf16[4096,1024]{1,0:T(8,128)(2,1)}), bf16[512,1024]{1,0:T(8,128)(2,1)}) %reduce-scatter.32.cloned.1.call-update) | async-done | bytes 1048592 | tf_op jit(solution)/shard_map/reduce_scatter | solution.py:289
  1490.6 77.9 %reduce-scatter.22.cloned.1.call-done = bf16[96,2048]{1,0:T(8,128)(2,1)} async-done(((bf16[768,2048]{1,0:T(8,128)(2,1)}), bf16[96,2048]{1,0:T(8,128)(2,1)}) %reduce-scatter.22.cloned.1.call-update) | async-done | bytes 393232 | tf_op jit(solution)/shard_map/reduce_scatter | solution.py:274
  1568.4 121.2 %reduce-scatter.26.cloned.1.call-done = bf16[128,3072]{1,0:T(8,128)(2,1)} async-done(((bf16[1024,3072]{1,0:T(8,128)(2,1)}), bf16[128,3072]{1,0:T(8,128)(2,1)}) %reduce-scatter.26.cloned.1.call-update) | async-done | bytes 786448 | tf_op jit(solution)/shard_map/reduce_scatter | solution.py:280
  1689.7 8.3 fusion.108
  1699.4 119.4 %all-reduce.7.cloned.1.call-done = f32[8,6144]{1,0:T(8,128)} async-done(((f32[8,6144]{1,0:T(8,128)}), f32[8,6144]{1,0:T(8,128)}) %all-reduce.7.cloned.1.call-update) | async-done | bytes 196624 | tf_op jit(solution)/shard_map/psum | solution.py:253
  1822.9 15.3 all-gather.30.cloned.1.call-done
  1840.5 80.6 %all-reduce.9.cloned.1.call-done = (bf16[96,2048]{1,0:T(8,128)(2,1)}, bf16[128,1024]{1,0:T(8,128)(2,1)}, bf16[128,3072]{1,0:T(8,128)(2,1)}, bf16[128,1024]{1,0:T...) async-done(((bf16[96,2048]{1,0:T(8,128)(2,1)}, bf16[128,1024]{1,0:T(8,128)(2,1)}, bf16[128,3072]{1,0:T(8,128)(2,1)}, bf16[128,1024]{1,0:T(8,128)(2,1)}, ...) | async-done | bytes 3801104 | tf_op jit(solution)/shard_map/psum | solution.py:295
  (439 shorter events, 255.4 us)
Async XLA Ops:
  7.2 77.5 %all-reduce.5.cloned.1.call-start = ((), (), s32[]{:S(2)}) async-start(), calls=%async_computation.11 | async-start | bytes 393216 | tf_op jit(solution)/shard_map/psum | solution.py:148
  9.8 125.6 %all-gather.12.cloned.1.call-start = ((), (), s32[]{:S(2)}) async-start(), calls=%async_computation.12 | async-start | bytes 2359296 | tf_op jit(solution)/shard_map/all_gather | solution.py:139
  10.6 186.2 %all-gather.14.cloned.1.call-start = ((), (), s32[]{:S(2)}) async-start(), calls=%async_computation.13 | async-start | bytes 3538944 | tf_op jit(solution)/shard_map/all_gather | solution.py:140
  11.3 235.6 %all-gather.16.cloned.1.call-start = ((), (), s32[]{:S(2)}) async-start(), calls=%async_computation.14 | async-start | bytes 2359296 | tf_op jit(solution)/shard_map/all_gather | solution.py:141
  11.9 334.9 %all-gather.18.cloned.1.call-start = ((), (), s32[]{:S(2)}) async-start(), calls=%async_computation.15 | async-start | bytes 7077888 | tf_op jit(solution)/shard_map/all_gather | solution.py:142
  12.5 361.1 %all-gather.20.cloned.1.call-start = ((), (), s32[]{:S(2)}) async-start(), calls=%async_computation.16 | async-start | bytes 2621440 | tf_op jit(solution)/shard_map/all_gather | solution.py:175
  85.7 261.1 %copy-start.41 = (f32[1,1024]{1,0:T(1,128)}, f32[1,1024]{1,0:T(1,128)S(1)}, u32[]{:S(2)}) copy-start(f32[1,1024]{1,0:T(1,128)S(1)} %get-tuple-element.333) | copy-start | bytes 12292
  85.7 490.5 %copy-start.42 = (f32[1,1024]{1,0:T(1,128)}, f32[1,1024]{1,0:T(1,128)S(1)}, u32[]{:S(2)}) copy-start(f32[1,1024]{1,0:T(1,128)S(1)} %get-tuple-element.337) | copy-start | bytes 12292
  85.7 628.4 %copy-start.39 = (f32[1,1024]{1,0:T(1,128)}, f32[1,1024]{1,0:T(1,128)S(1)}, u32[]{:S(2)}) copy-start(f32[1,1024]{1,0:T(1,128)S(1)} %get-tuple-element.332) | copy-start | bytes 12292
  249.6 608.1 %copy-start.52 = (f32[256]{0:T(256)}, f32[256]{0:T(256)S(1)}, u32[]{:S(2)}) copy-start(f32[256]{0:T(256)S(1)} %broadcast_multiply_fusion.1) | copy-start | bytes 3076
  249.9 607.8 %copy-start.58 = (f32[256]{0:T(256)}, f32[256]{0:T(256)S(1)}, u32[]{:S(2)}) copy-start(f32[256]{0:T(256)S(1)} %fusion.150) | copy-start | bytes 3076
  352.7 45.8 %all-gather.22.cloned.1.call-start = ((), (), s32[]{:S(2)}) async-start(), calls=%async_computation.17 | async-start | bytes 2621440 | tf_op jit(solution)/shard_map/all_gather | solution.py:176
  353.4 96.9 %all-gather.24.cloned.1.call-start = ((), (), s32[]{:S(2)}) async-start(), calls=%async_computation.18 | async-start | bytes 2359296 | tf_op jit(solution)/shard_map/all_gather | solution.py:143
  354.2 222.0 %all-gather.26.cloned.1.call-start = ((), (), s32[]{:S(2)}) async-start(), calls=%async_computation.19 | async-start | bytes 9437184 | tf_op jit(solution)/shard_map/all_gather | solution.py:144
  354.9 346.6 %all-gather.28.cloned.1.call-start = ((), (), s32[]{:S(2)}) async-start(), calls=%async_computation.20 | async-start | bytes 9437184 | tf_op jit(solution)/shard_map/all_gather | solution.py:145
  355.5 448.1 %reduce-scatter.14.cloned.1.call-start = ((), (), s32[]{:S(2)}) async-start(), calls=%async_computation.22 | async-start | bytes 5242880 | tf_op jit(solution)/shard_map/reduce_scatter | solution.py:203
  453.0 261.1 %copy-start.53 = (f32[256]{0:T(256)}, f32[256]{0:T(256)S(1)}, u32[]{:S(2)}) copy-start(f32[256]{0:T(256)S(1)} %broadcast_multiply_fusion) | copy-start | bytes 3076
  454.2 259.9 %copy-start.59 = (f32[256]{0:T(256)}, f32[256]{0:T(256)S(1)}, u32[]{:S(2)}) copy-start(f32[256]{0:T(256)S(1)} %fusion.151) | copy-start | bytes 3076
  760.8 89.7 %reduce-scatter.12.cloned.1.call-start = ((), (), s32[]{:S(2)}) async-start(), calls=%async_computation.21 | async-start | bytes 5242880 | tf_op jit(solution)/shard_map/reduce_scatter | solution.py:202
  761.3 176.1 %reduce-scatter.20.cloned.1.call-start = ((), (), s32[]{:S(2)}) async-start(), calls=%async_computation.26 | async-start | bytes 2949120 | tf_op jit(solution)/shard_map/reduce_scatter | solution.py:220
  904.2 68.7 %reduce-scatter.18.cloned.1.call-start = ((), (), s32[]{:S(2)}) async-start(), calls=%async_computation.25 | async-start | bytes 2949120 | tf_op jit(solution)/shard_map/reduce_scatter | solution.py:217
  904.8 140.1 %reduce-scatter.16.cloned.1.call-start = ((), (), s32[]{:S(2)}) async-start(), calls=%async_computation.24 | async-start | bytes 2359296 | tf_op jit(solution)/shard_map/reduce_scatter | solution.py:271
  908.5 207.0 %reduce-scatter.28.cloned.1.call-start = ((), (), s32[]{:S(2)}) async-start(), calls=%async_computation.30 | async-start | bytes 2359296 | tf_op jit(solution)/shard_map/reduce_scatter | solution.py:283
  912.3 274.5 %reduce-scatter.24.cloned.1.call-start = ((), (), s32[]{:S(2)}) async-start(), calls=%async_computation.28 | async-start | bytes 2359296 | tf_op jit(solution)/shard_map/reduce_scatter | solution.py:277
  915.9 423.0 %reduce-scatter.30.cloned.1.call-start = ((), (), s32[]{:S(2)}) async-start(), calls=%async_computation.31 | async-start | bytes 9437184 | tf_op jit(solution)/shard_map/reduce_scatter | solution.py:286
  923.7 566.9 %reduce-scatter.32.cloned.1.call-start = ((), (), s32[]{:S(2)}) async-start(), calls=%async_computation.32 | async-start | bytes 9437184 | tf_op jit(solution)/shard_map/reduce_scatter | solution.py:289
  932.4 636.0 %reduce-scatter.22.cloned.1.call-start = ((), (), s32[]{:S(2)}) async-start(), calls=%async_computation.27 | async-start | bytes 3538944 | tf_op jit(solution)/shard_map/reduce_scatter | solution.py:274
  982.9 706.8 %reduce-scatter.26.cloned.1.call-start = ((), (), s32[]{:S(2)}) async-start(), calls=%async_computation.29 | async-start | bytes 7077888 | tf_op jit(solution)/shard_map/reduce_scatter | solution.py:280
  989.1 700.5 %copy-start.5 = (f32[256,1024]{1,0:T(8,128)S(1)}, f32[256,1024]{1,0:T(8,128)}, u32[]{:S(2)}) copy-start(f32[256,1024]{1,0:T(8,128)} %copy-done.3) | copy-start | bytes 3145732
  989.2 829.7 %all-reduce.7.cloned.1.call-start = ((), (), s32[]{:S(2)}) async-start(), calls=%async_computation.23 | async-start | bytes 393216 | tf_op jit(solution)/shard_map/psum | solution.py:253
  995.4 842.8 %all-gather.30.cloned.1.call-start = ((), (), s32[]{:S(2)}) async-start(), calls=%async_computation.33 | async-start | bytes 1310720 | tf_op jit(solution)/shard_map/all_gather | solution.py:15
  1044.9 876.2 %all-reduce.9.cloned.1.call-start = ((), (), s32[]{:S(2)}) async-start(), calls=%async_computation.34 | async-start | bytes 7602176 | tf_op jit(solution)/shard_map/psum | solution.py:295
  (99 other events, 1510.2 us)
Sparse Core Ops, SparseCore 0:
  11.9 72.7 all-reduce.4
  87.1 48.3 all-gather.11
  137.9 58.9 all-gather.13
  199.0 47.9 all-gather.15
  249.2 97.5 all-gather.17
  352.8 20.7 all-gather.19
  375.8 22.5 all-gather.21
  400.8 49.5 all-gather.23
  452.7 123.4 all-gather.25
  578.4 123.1 all-gather.27
  760.9 42.6 reduce-scatter.13
  806.0 44.4 reduce-scatter.11
  904.4 33.0 reduce-scatter.19
  939.8 33.0 reduce-scatter.17
  977.3 67.5 reduce-scatter.15
  1048.7 66.7 reduce-scatter.27
  1119.9 66.8 reduce-scatter.23
  1190.7 148.0 reduce-scatter.29
  1342.5 148.0 reduce-scatter.31
  1495.0 73.3 reduce-scatter.21
  1572.4 117.1 reduce-scatter.25
  1696.7 122.1 all-reduce.6
  1820.5 17.6 all-gather.29
  1841.0 80.0 all-reduce.8
